TPU v7x, 256 devices: a whole 4x4x8 slice. The times are simulated.
256 devices in a mesh: dp: 4 (over z_lo), ctx: 64 (over z_hi, x, y, core).
Axes of the slice: x: 4, y: 4, z: 8 (z_hi: 2, z_lo: 4; z = z_hi * 4 + z_lo), core: 2. Of those that a mesh axis runs over, the one named last changes fastest.
Arguments:
- inputs: bfloat16 [4, 131072, 256], P('dp', 'ctx'), may hold values from -16 to 16
- grad_out: bfloat16 [4, 131072, 256], P('dp', 'ctx'), may hold values from -6 to 6
- w_in: bfloat16 [256, 768], replicated, may hold values from -0.375 to 0.375
- filter_real: float32 [512, 512, 16], P('ctx'), may hold values from -12 to 12, as said below
- filter_imag: float32 [512, 512, 16], P('ctx'), may hold values from -12 to 12, as said below
Outputs:
- gated_out: bfloat16 [4, 131072, 256], P('dp', 'ctx')
- grad_w_in: float32 [256, 768], P('dp')
Inputs may be any that keep to these rules, and one draw needn't show every extreme that they name: Each long filter is real: with P = 262144, filter_real at frequency (P - f) mod P equals filter_real at frequency f. Each long filter is real: with P = 262144, filter_imag at frequency (P - f) mod P is minus filter_imag at frequency f.
All inputs are finite; a program needn't handle non-finite values.
Results may differ from a plain program's by a relative error of at most 0.011.
Values may be sent and summed in bfloat16 or wider, within the bound.
A program may use at most 128 MiB of HBM per device.

v0:
```python
import math

import jax
import jax.numpy as jnp
from jax import lax
from jax.sharding import PartitionSpec as P

N1 = 512
N2 = 512


def dft_tables(row_index, col_index, period, factor):
    phase_angle = (row_index[:, None] * col_index[None, :] % period).astype(jnp.float32) * (
        2.0 * math.pi / period
    )
    return (
        (jnp.cos(phase_angle) * factor).astype(jnp.bfloat16),
        (jnp.sin(phase_angle) * factor).astype(jnp.bfloat16),
    )


def twiddle_tables(row_index, col_index, period):
    phase_angle = (row_index[:, None] * col_index[None, :] % period).astype(jnp.float32) * (
        2.0 * math.pi / period
    )
    return (jnp.cos(phase_angle)[:, :, None], jnp.sin(phase_angle)[:, :, None])


def combine(cos_part, sin_part, orient):
    real_part = cos_part[:, :, 0] - orient * sin_part[:, :, 1]
    imag_part = cos_part[:, :, 1] + orient * sin_part[:, :, 0]
    return (real_part, imag_part)


def rotate(real_part, imag_part, cos_table, sin_table, orient):
    new_real = real_part * cos_table - orient * imag_part * sin_table
    new_imag = imag_part * cos_table + orient * real_part * sin_table
    return (new_real, new_imag)


def pack_complex(real_part, imag_part):
    return jnp.stack([real_part, imag_part], axis=2).astype(jnp.bfloat16)


def long_conv(signal, spec_real, spec_imag, tables):
    cos_one, sin_one, cos_two, sin_two, fwd_cos, fwd_sin, inv_cos, inv_sin = tables
    block_data = lax.all_to_all(signal, "ctx", split_axis=1, concat_axis=0, tiled=True)
    cos_part = jnp.einsum("ft,tcpm->fcpm", cos_one, block_data, preferred_element_type=jnp.float32)
    sin_part = jnp.einsum("ft,tcpm->fcpm", sin_one, block_data, preferred_element_type=jnp.float32)
    real_part, imag_part = combine(cos_part, sin_part, -1.0)
    real_part, imag_part = rotate(real_part, imag_part, fwd_cos, fwd_sin, -1.0)
    spectrum = pack_complex(real_part, imag_part)
    columns = lax.all_to_all(spectrum, "ctx", split_axis=0, concat_axis=1, tiled=True)
    cos_part = jnp.einsum("fcpm,cg->fgpm", columns, cos_two, preferred_element_type=jnp.float32)
    sin_part = jnp.einsum("fcpm,cg->fgpm", columns, sin_two, preferred_element_type=jnp.float32)
    real_part, imag_part = combine(cos_part, sin_part, -1.0)
    prod_real = real_part * spec_real - imag_part * spec_imag
    prod_imag = real_part * spec_imag + imag_part * spec_real
    product = pack_complex(prod_real, prod_imag)
    cos_part = jnp.einsum("fgpm,gc->fcpm", product, cos_two, preferred_element_type=jnp.float32)
    sin_part = jnp.einsum("fgpm,gc->fcpm", product, sin_two, preferred_element_type=jnp.float32)
    real_part, imag_part = combine(cos_part, sin_part, 1.0)
    real_part, imag_part = rotate(real_part, imag_part, inv_cos, inv_sin, 1.0)
    returned = pack_complex(real_part, imag_part)
    block_data = lax.all_to_all(returned, "ctx", split_axis=1, concat_axis=0, tiled=True)
    cos_part = jnp.einsum("ft,fcpm->tcpm", cos_one, block_data, preferred_element_type=jnp.float32)
    sin_part = jnp.einsum("ft,fcpm->tcpm", sin_one, block_data, preferred_element_type=jnp.float32)
    real_part, imag_part = combine(cos_part, sin_part, 1.0)
    restored = pack_complex(real_part, imag_part)
    return lax.all_to_all(restored, "ctx", split_axis=0, concat_axis=1, tiled=True)


def per_device(inputs, grad_out, w_in, filter_real, filter_imag):
    ctx_count = lax.axis_size("ctx")
    ctx_pos = lax.axis_index("ctx")
    group_count = lax.axis_size("dp")
    tokens = inputs[0]
    cotangent = grad_out[0]
    tok_rows, chan_total = tokens.shape
    chan_half = chan_total // 2
    period = N1 * N2
    seq_len = period // 2
    row_count = N1 // ctx_count
    col_count = N2 // ctx_count
    shard_rows = tok_rows // N2
    full_index = jnp.arange(N1, dtype=jnp.int32)
    half_index = jnp.arange(N1 // 2, dtype=jnp.int32)
    second_index = jnp.arange(N2, dtype=jnp.int32)
    local_rows = ctx_pos * row_count + jnp.arange(row_count, dtype=jnp.int32)
    local_cols = ctx_pos * col_count + jnp.arange(col_count, dtype=jnp.int32)
    cos_one, sin_one = dft_tables(full_index, half_index, N1, 1.0 / math.sqrt(N1))
    cos_two, sin_two = dft_tables(second_index, second_index, N2, 1.0 / math.sqrt(N2))
    fwd_cos, fwd_sin = twiddle_tables(full_index, local_cols, period)
    inv_cos, inv_sin = twiddle_tables(local_rows, second_index, period)
    tables = (cos_one, sin_one, cos_two, sin_two, fwd_cos, fwd_sin, inv_cos, inv_sin)
    repeats = chan_half // filter_real.shape[2]
    tiled_real = jnp.tile(filter_real, (1, 1, repeats))
    tiled_imag = jnp.tile(filter_imag, (1, 1, repeats))
    features = jnp.dot(tokens, w_in, preferred_element_type=jnp.float32).astype(jnp.bfloat16)
    gate_part = features[:, :chan_total]
    key_part = features[:, chan_total : 2 * chan_total]
    value_part = features[:, 2 * chan_total :]
    mixed = (key_part.astype(jnp.float32) * value_part.astype(jnp.float32)).astype(jnp.bfloat16)
    grad_smooth = (cotangent.astype(jnp.float32) * gate_part.astype(jnp.float32)).astype(
        jnp.bfloat16
    )
    mixed_grid = mixed.reshape(shard_rows, N2, 2, chan_half)
    grad_grid = grad_smooth.reshape(shard_rows, N2, 2, chan_half)
    smooth_grid = long_conv(mixed_grid, tiled_real, tiled_imag, tables)
    back_grid = long_conv(grad_grid, tiled_real, -tiled_imag, tables)
    smooth = smooth_grid.reshape(tok_rows, chan_total).astype(jnp.float32)
    gated = (gate_part.astype(jnp.float32) * smooth).astype(jnp.bfloat16)
    grad_gate = (cotangent.astype(jnp.float32) * smooth).astype(jnp.bfloat16)
    grad_mixed = back_grid.reshape(tok_rows, chan_total).astype(jnp.float32)
    grad_key = (grad_mixed * value_part.astype(jnp.float32)).astype(jnp.bfloat16)
    grad_value = (grad_mixed * key_part.astype(jnp.float32)).astype(jnp.bfloat16)
    grad_features = jnp.concatenate([grad_gate, grad_key, grad_value], axis=1)
    scale = 1.0 / math.sqrt(inputs.shape[0] * group_count * seq_len)
    share_rows = chan_total // group_count
    full_term = lax.dot_general(
        tokens, grad_features, (((0,), (0,)), ((), ())), preferred_element_type=jnp.float32
    )
    everything = lax.psum(full_term, ("dp", "ctx"))
    summed = lax.dynamic_slice_in_dim(everything, lax.axis_index("dp") * share_rows, share_rows, 0)
    return (gated[None], summed * scale)


def solution(mesh):
    placed = (
        P("dp", "ctx", None),
        P("dp", "ctx", None),
        P(),
        P("ctx", None, None),
        P("ctx", None, None),
    )
    return jax.shard_map(
        per_device,
        mesh=mesh,
        in_specs=placed,
        out_specs=(P("dp", "ctx", None), P("dp", None)),
        check_vma=False,
    )
```

profile of v0, /device:TPU:1, one launch (start us, length us, event | category | flops | bytes accessed | tf_op | source)
XLA Modules:
  0.0 739.4 jit_solution(1599978977401689452)
XLA Ops:
  9.9 2.3 fusion.11
  14.0 2.3 copy.105
  16.3 15.6 %all-to-all-start.4 = ((bf16[4,512,2,128]{3,2,0,1:T(2,128)(2,1)}), bf16[4,512,2,128]{3,2,0,1:T(2,128)(2,1)S(1)}, u32[]{:S(2)}, u32[]{:S(2)}) async-start(bf16[4,512,2,128]{3,2,0,1:T(2,128)(2,1)} %copy.105), calls=%async_computation.4 | async-start | bytes 2097152 | tf_op jit(solution)/shard_map/all_to_all | solution.py:47
  31.9 2.6 reshape.183
  34.6 3.8 copy.86
  38.4 17.0 %all-to-all-done.4 = bf16[4,512,2,128]{3,2,0,1:T(2,128)(2,1)S(1)} async-done(((bf16[4,512,2,128]{3,2,0,1:T(2,128)(2,1)}), bf16[4,512,2,128]{3,2,0,1:T(2,128)(2,1)S(1)}, u32[]{:S(2)}, u32[]{:S(2)}) %all-to-all-start.4) | async-done | bytes 1048608 | tf_op jit(solution)/shard_map/all_to_all | solution.py:47
  55.4 12.9 %all-to-all-start = ((bf16[4,512,2,128]{3,2,0,1:T(2,128)(2,1)}), bf16[4,512,2,128]{3,2,0,1:T(2,128)(2,1)}, u32[]{:S(2)}, u32[]{:S(2)}) async-start(bf16[4,512,2,128]{3,2,0,1:T(2,128)(2,1)} %copy.86), calls=%async_computation | async-start | bytes 2097152 | tf_op jit(solution)/shard_map/all_to_all | solution.py:47
  69.4 4.2 fusion.74
  73.6 4.1 fusion.80
  77.8 11.5 %all-to-all-done = bf16[4,512,2,128]{3,2,0,1:T(2,128)(2,1)} async-done(((bf16[4,512,2,128]{3,2,0,1:T(2,128)(2,1)}), bf16[4,512,2,128]{3,2,0,1:T(2,128)(2,1)}, u32[]{:S(2)}, u32[]{:S(2)}) %all-to-all-start) | async-done | bytes 1048608 | tf_op jit(solution)/shard_map/all_to_all | solution.py:47
  91.5 2.6 fusion.78
  94.1 2.6 fusion.82
  96.7 3.4 subtract_convert_fusion.2
  100.3 3.5 copy.91
  103.8 15.6 %all-to-all-start.1 = ((bf16[512,8,2,128]{3,2,1,0:T(2,128)(2,1)}), bf16[512,8,2,128]{3,2,1,0:T(2,128)(2,1)}, u32[]{:S(2)}, u32[]{:S(2)}) async-start(bf16[512,8,2,128]{3,2,1,0:T(2,128)(2,1)} %copy.91), calls=%async_computation.1 | async-start | bytes 4194304 | tf_op jit(solution)/shard_map/all_to_all | solution.py:53
  120.8 3.5 copy.110
  124.3 26.6 %all-to-all-done.1 = bf16[512,8,2,128]{3,2,1,0:T(2,128)(2,1)} async-done(((bf16[512,8,2,128]{3,2,1,0:T(2,128)(2,1)}), bf16[512,8,2,128]{3,2,1,0:T(2,128)(2,1)}, u32[]{:S(2)}, u32[]{:S(2)}) %all-to-all-start.1) | async-done | bytes 2097184 | tf_op jit(solution)/shard_map/all_to_all | solution.py:53
  150.9 27.7 %all-to-all-start.5 = ((bf16[512,8,2,128]{3,2,1,0:T(2,128)(2,1)}), bf16[512,8,2,128]{3,2,1,0:T(2,128)(2,1)}, u32[]{:S(2)}, u32[]{:S(2)}) async-start(bf16[512,8,2,128]{3,2,1,0:T(2,128)(2,1)} %copy.110), calls=%async_computation.5 | async-start | bytes 4194304 | tf_op jit(solution)/shard_map/all_to_all | solution.py:53
  180.3 2.9 copy.93
  184.9 2.9 copy.94
  187.9 8.2 %convolution_bitcast_fusion.6 = f32[8,512,2,128]{3,1,2,0:T(8,128)} fusion(bf16[64,8,8,2,128]{4,3,2,1,0:T(2,128)(2,1)} %bitcast.11), kind=kOutput, calls=%fused_computation.19 | convolution fusion | flops 1077936128 | bytes 6291456 | tf_op jit(solution)/shard_map/fcpm,cg->fgpm/dot_general | solution.py:55
  196.1 8.5 %convolution_bitcast_fusion.7 = f32[8,512,2,128]{3,1,2,0:T(8,128)} fusion(bf16[64,8,8,2,128]{4,3,2,1,0:T(2,128)(2,1)} %bitcast.11), kind=kOutput, calls=%fused_computation.20 | convolution fusion | flops 1077936128 | bytes 6291456 | tf_op jit(solution)/shard_map/fcpm,cg->fgpm/dot_general | solution.py:54
  204.6 5.6 all-to-all-done.5
  210.2 6.7 convolution_bitcast_fusion.2
  216.9 6.7 convolution_bitcast_fusion.3
  225.7 4.9 convolution_bitcast_fusion.5
  230.6 4.9 convolution_bitcast_fusion.4
  235.5 5.1 convolution_bitcast_fusion.1
  240.5 4.9 convolution_bitcast_fusion
  245.4 3.0 subtract_convert_fusion
  248.7 3.5 copy.97
  252.2 28.3 %all-to-all-start.2 = ((bf16[8,512,2,128]{3,2,0,1:T(2,128)(2,1)}), bf16[8,512,2,128]{3,2,0,1:T(2,128)(2,1)}, u32[]{:S(2)}, u32[]{:S(2)}) async-start(bf16[8,512,2,128]{3,2,0,1:T(2,128)(2,1)} %copy.97), calls=%async_computation.2 | async-start | bytes 4194304 | tf_op jit(solution)/shard_map/all_to_all | solution.py:65
  282.0 3.5 copy.115
  285.4 26.4 %all-to-all-done.2 = bf16[8,512,2,128]{3,2,0,1:T(2,128)(2,1)} async-done(((bf16[8,512,2,128]{3,2,0,1:T(2,128)(2,1)}), bf16[8,512,2,128]{3,2,0,1:T(2,128)(2,1)}, u32[]{:S(2)}, u32[]{:S(2)}) %all-to-all-start.2) | async-done | bytes 2097184 | tf_op jit(solution)/shard_map/all_to_all | solution.py:65
  311.9 27.7 %all-to-all-start.6 = ((bf16[8,512,2,128]{3,2,0,1:T(2,128)(2,1)}), bf16[8,512,2,128]{3,2,0,1:T(2,128)(2,1)}, u32[]{:S(2)}, u32[]{:S(2)}) async-start(bf16[8,512,2,128]{3,2,0,1:T(2,128)(2,1)} %copy.115), calls=%async_computation.6 | async-start | bytes 4194304 | tf_op jit(solution)/shard_map/all_to_all | solution.py:65
  339.6 4.2 fusion.26
  343.8 4.2 fusion.28
  350.4 20.7 %all-to-all-done.6 = bf16[8,512,2,128]{3,2,0,1:T(2,128)(2,1)} async-done(((bf16[8,512,2,128]{3,2,0,1:T(2,128)(2,1)}), bf16[8,512,2,128]{3,2,0,1:T(2,128)(2,1)}, u32[]{:S(2)}, u32[]{:S(2)}) %all-to-all-start.6) | async-done | bytes 2097184 | tf_op jit(solution)/shard_map/all_to_all | solution.py:65
  371.1 27.8 %all-to-all-start.3 = ((bf16[256,8,2,128]{3,2,1,0:T(2,128)(2,1)}), bf16[256,8,2,128]{3,2,1,0:T(2,128)(2,1)S(1)}, u32[]{:S(2)}, u32[]{:S(2)}) async-start(bf16[256,8,2,128]{3,2,1,0:T(2,128)(2,1)} %copy.99), calls=%async_computation.3 | async-start | bytes 2097152 | tf_op jit(solution)/shard_map/all_to_all | solution.py:70
  398.9 4.2 fusion.20
  403.1 4.2 fusion.22
  409.7 10.4 %all-to-all-done.3 = bf16[256,8,2,128]{3,2,1,0:T(2,128)(2,1)S(1)} async-done(((bf16[256,8,2,128]{3,2,1,0:T(2,128)(2,1)}), bf16[256,8,2,128]{3,2,1,0:T(2,128)(2,1)S(1)}, u32[]{:S(2)}, u32[]{:S(2)}) %all-to-all-start.3) | async-done | bytes 1048608 | tf_op jit(solution)/shard_map/all_to_all | solution.py:70
  420.1 15.5 %all-to-all-start.7 = ((bf16[256,8,2,128]{3,2,1,0:T(2,128)(2,1)}), bf16[256,8,2,128]{3,2,1,0:T(2,128)(2,1)}, u32[]{:S(2)}, u32[]{:S(2)}) async-start(bf16[256,8,2,128]{3,2,1,0:T(2,128)(2,1)} %copy.117), calls=%async_computation.7 | async-start | bytes 2097152 | tf_op jit(solution)/shard_map/all_to_all | solution.py:70
  437.5 2.9 copy.102
  440.4 16.3 %all-to-all-done.7 = bf16[256,8,2,128]{3,2,1,0:T(2,128)(2,1)} async-done(((bf16[256,8,2,128]{3,2,1,0:T(2,128)(2,1)}), bf16[256,8,2,128]{3,2,1,0:T(2,128)(2,1)}, u32[]{:S(2)}, u32[]{:S(2)}) %all-to-all-start.7) | async-done | bytes 1048608 | tf_op jit(solution)/shard_map/all_to_all | solution.py:70
  459.9 2.9 copy.120
  462.8 4.4 fusion.9
  470.4 260.0 %all-reduce.2.cloned.1.call-done = f32[256,768]{0,1:T(8,128)} async-done(((f32[256,768]{0,1:T(8,128)}), f32[256,768]{0,1:T(8,128)}) %all-reduce.2.cloned.1.call-update) | async-done | bytes 786448 | tf_op jit(solution)/shard_map/psum | solution.py:123
  (57 shorter events, 31.6 us)
Async XLA Ops:
  7.2 1.6 copy-start
  7.2 1.6 copy-start.8
  9.8 2.3 copy-start.1
  16.3 39.1 %all-to-all-start.4 = ((bf16[4,512,2,128]{3,2,0,1:T(2,128)(2,1)}), bf16[4,512,2,128]{3,2,0,1:T(2,128)(2,1)S(1)}, u32[]{:S(2)}, u32[]{:S(2)}) async-start(bf16[4,512,2,128]{3,2,0,1:T(2,128)(2,1)} %copy.105), calls=%async_computation.4 | async-start | bytes 2097152 | tf_op jit(solution)/shard_map/all_to_all | solution.py:47
  55.4 33.9 %all-to-all-start = ((bf16[4,512,2,128]{3,2,0,1:T(2,128)(2,1)}), bf16[4,512,2,128]{3,2,0,1:T(2,128)(2,1)}, u32[]{:S(2)}, u32[]{:S(2)}) async-start(bf16[4,512,2,128]{3,2,0,1:T(2,128)(2,1)} %copy.86), calls=%async_computation | async-start | bytes 2097152 | tf_op jit(solution)/shard_map/all_to_all | solution.py:47
  91.5 5.2 copy-start.3
  94.1 2.6 copy-start.2
  103.8 47.2 %all-to-all-start.1 = ((bf16[512,8,2,128]{3,2,1,0:T(2,128)(2,1)}), bf16[512,8,2,128]{3,2,1,0:T(2,128)(2,1)}, u32[]{:S(2)}, u32[]{:S(2)}) async-start(bf16[512,8,2,128]{3,2,1,0:T(2,128)(2,1)} %copy.91), calls=%async_computation.1 | async-start | bytes 4194304 | tf_op jit(solution)/shard_map/all_to_all | solution.py:53
  124.3 54.3 %copy-start.9 = (f32[8,512,16]{1,2,0:T(8,128)S(1)}, f32[8,512,16]{1,2,0:T(8,128)}, u32[]{:S(2)}) copy-start(f32[8,512,16]{1,2,0:T(8,128)} %param.8) | copy-start | bytes 786436
  150.9 59.3 %all-to-all-start.5 = ((bf16[512,8,2,128]{3,2,1,0:T(2,128)(2,1)}), bf16[512,8,2,128]{3,2,1,0:T(2,128)(2,1)}, u32[]{:S(2)}, u32[]{:S(2)}) async-start(bf16[512,8,2,128]{3,2,1,0:T(2,128)(2,1)} %copy.110), calls=%async_computation.5 | async-start | bytes 4194304 | tf_op jit(solution)/shard_map/all_to_all | solution.py:53
  180.3 3.0 copy-start.10
  210.2 13.4 %copy-start.7 = (f32[8,512,2,128]{3,1,2,0:T(8,128)S(1)}, f32[8,512,2,128]{3,1,2,0:T(8,128)}, u32[]{:S(2)}) copy-start(f32[8,512,2,128]{3,1,2,0:T(8,128)} %convolution_bitcast_fusion.7) | copy-start | bytes 12582916
  216.9 6.7 copy-start.4
  216.9 6.7 copy-start.5
  216.9 6.7 copy-start.6
  252.2 59.7 %all-to-all-start.2 = ((bf16[8,512,2,128]{3,2,0,1:T(2,128)(2,1)}), bf16[8,512,2,128]{3,2,0,1:T(2,128)(2,1)}, u32[]{:S(2)}, u32[]{:S(2)}) async-start(bf16[8,512,2,128]{3,2,0,1:T(2,128)(2,1)} %copy.97), calls=%async_computation.2 | async-start | bytes 4194304 | tf_op jit(solution)/shard_map/all_to_all | solution.py:65
  311.9 59.3 %all-to-all-start.6 = ((bf16[8,512,2,128]{3,2,0,1:T(2,128)(2,1)}), bf16[8,512,2,128]{3,2,0,1:T(2,128)(2,1)}, u32[]{:S(2)}, u32[]{:S(2)}) async-start(bf16[8,512,2,128]{3,2,0,1:T(2,128)(2,1)} %copy.115), calls=%async_computation.6 | async-start | bytes 4194304 | tf_op jit(solution)/shard_map/all_to_all | solution.py:65
  371.1 49.0 %all-to-all-start.3 = ((bf16[256,8,2,128]{3,2,1,0:T(2,128)(2,1)}), bf16[256,8,2,128]{3,2,1,0:T(2,128)(2,1)S(1)}, u32[]{:S(2)}, u32[]{:S(2)}) async-start(bf16[256,8,2,128]{3,2,1,0:T(2,128)(2,1)} %copy.99), calls=%async_computation.3 | async-start | bytes 2097152 | tf_op jit(solution)/shard_map/all_to_all | solution.py:70
  420.1 36.6 %all-to-all-start.7 = ((bf16[256,8,2,128]{3,2,1,0:T(2,128)(2,1)}), bf16[256,8,2,128]{3,2,1,0:T(2,128)(2,1)}, u32[]{:S(2)}, u32[]{:S(2)}) async-start(bf16[256,8,2,128]{3,2,1,0:T(2,128)(2,1)} %copy.117), calls=%async_computation.7 | async-start | bytes 2097152 | tf_op jit(solution)/shard_map/all_to_all | solution.py:70
  435.6 294.8 %all-reduce.2.cloned.1.call-start = ((), (), s32[]{:S(2)}) async-start(), calls=%async_computation.8 | async-start | bytes 1572864 | tf_op jit(solution)/shard_map/psum | solution.py:123
Sparse Core Ops, SparseCore 0:
  469.2 261.1 all-reduce.1
where the time goes:
time: 746 us; the launch traced here: 739 us
  waiting for transfers between devices  395 us (53%)
  starting transfers between devices  171 us (23%)
  matrix products  82.9 us (11%)
  local copies, waits for them, and re-layouts  55.1 us (7%)
  other arithmetic  21 us (3%)
  between operations  14.7 us (2%)
    psum x1, waiting for transfers between devices, per_device(): everything = lax.psum(full_term, ('dp', 'ctx'))  260 us
    all_to_all x2, starting transfers between devices, long_conv(): lax.all_to_all(returned, 'ctx', split_axis=1, concat_axis=0, tiled=True)  56 us
    all_to_all x2, waiting for transfers between devices, long_conv(): lax.all_to_all(returned, 'ctx', split_axis=1, concat_axis=0, tiled=True)  47.2 us
    all_to_all x2, starting transfers between devices, long_conv(): lax.all_to_all(spectrum, 'ctx', split_axis=0, concat_axis=1, tiled=True)  43.3 us
    all_to_all x2, starting transfers between devices, long_conv(): lax.all_to_all(restored, 'ctx', split_axis=0, concat_axis=1, tiled=True)  43.3 us
    all_to_all x2, waiting for transfers between devices, long_conv(): lax.all_to_all(spectrum, 'ctx', split_axis=0, concat_axis=1, tiled=True)  32.2 us
    all_to_all x2, starting transfers between devices, long_conv(): lax.all_to_all(signal, 'ctx', split_axis=1, concat_axis=0, tiled=True)  28.5 us
    all_to_all x2, waiting for transfers between devices, long_conv(): lax.all_to_all(signal, 'ctx', split_axis=1, concat_axis=0, tiled=True)  28.5 us
  transfers between devices with their start and end apart: 9, of which 9 were waited for; matrix products, arithmetic and copies ran while one was open for 11% of the time, Pallas kernels for 0%

commit v1 on v0

v1 whole, which is shorter than its diff:
```python
import math

import jax
import jax.numpy as jnp
import numpy as np
from jax import lax
from jax.experimental import pallas as pl
from jax.experimental.pallas import tpu as pltpu
from jax.sharding import PartitionSpec as P

N1 = 512
N2 = 512
ROWS = 272
NCH = 2
MESH = pl.DeviceIdType.MESH
BF = jnp.bfloat16
F32 = jnp.float32


def tables():
    half = N1 // 2
    period = N1 * N2
    t1 = np.arange(half)
    fwd = np.zeros((2, 2 * ROWS, half), np.float64)
    inv = np.zeros((2, half, 2 * ROWS), np.float64)
    base = np.zeros((2, ROWS // 8), np.int64)
    for zh in range(2):
        rows = np.concatenate(
            [zh * half + np.arange(half), (1 - zh) * half + np.arange(8), np.zeros(8, np.int64)]
        )
        base[zh] = rows[::8]
        angle = 2.0 * np.pi * ((rows[:, None] * t1[None, :]) % N1) / N1
        scale = 1.0 / math.sqrt(N1)
        cos = (np.cos(angle) * scale).astype(BF).astype(np.float64)
        sin = (np.sin(angle) * scale).astype(BF).astype(np.float64)
        cos[half + 8 :] = 0.0
        sin[half + 8 :] = 0.0
        fwd[zh, :ROWS] = cos
        fwd[zh, ROWS:] = -sin
        weight = np.where((rows == 0) | (rows == half), 1.0, 2.0)
        weight[half + 1 :] = 0.0
        inv[zh, :, :ROWS] = (weight[:, None] * cos).T
        inv[zh, :, ROWS:] = -(weight[:, None] * sin).T
    t2 = np.arange(N2)
    angle = 2.0 * np.pi * ((t2[:, None] * t2[None, :]) % N2) / N2
    cos2 = np.cos(angle) / math.sqrt(N2)
    sin2 = np.sin(angle) / math.sqrt(N2)
    two = np.stack([cos2, sin2, -sin2])
    coarse = 2.0 * np.pi * ((base[:, :, None] * t2) % period) / period
    fine = 2.0 * np.pi * ((np.arange(8)[:, None] * t2) % period) / period
    coarse = np.stack([np.cos(coarse), np.sin(coarse)], axis=1)[:, :, :, None, :]
    fine = np.stack([np.cos(fine), np.sin(fine)])
    order = np.arange(128)
    zh, g, i4 = order // 64, (order // 4) % 16, order % 4
    perm = np.zeros((128, 128))
    perm[order, zh * 64 + i4 * 16 + g] = 1.0
    return (
        fwd.astype(BF),
        inv.astype(BF),
        two.astype(BF),
        coarse.astype(np.float32),
        fine.astype(np.float32),
        perm.astype(BF),
        perm.T.copy().astype(BF),
        np.eye(256).astype(BF),
    )


def nt(a, b):
    return lax.dot_general(a, b, (((1,), (1,)), ((), ())), preferred_element_type=F32)


def nn(a, b):
    return jnp.dot(a, b, preferred_element_type=F32)


def mingle(a, b):
    low = lax.broadcasted_iota(jnp.int32, a.shape, 1) < 4
    first = jnp.where(low, a, pltpu.roll(b, 4, 1))
    second = jnp.where(low, pltpu.roll(a, 4, 1), b)
    return first, second


def kernel(
    x_ref, g_ref, w_ref, fr_in, fi_in, fwd_any, inv_any, two_any, coarse_ref, fine_ref,
    perm_ref, permt_ref, eye_ref,
    out_ref, grad_ref,
    fwd, inv, tab2, tab3, xt, wt, feat, gt, fsc, fsend, frecv, fre, fim, twc, tws,
    send_in, recv_in, mix, spec, prod, ret, send_out, recv_out,
    part, precv, zsend, zrecv, fin, frows,
    tab_sem, fsem_s, fsem_r, in_s, in_r, out_s, out_r, p_s, p_r, z_s, z_r, g_s, g_r,
):
    zl = lax.axis_index("dp")
    ctx = lax.axis_index("ctx")
    core = ctx % 2
    s = ctx % 32
    zh = ctx // 32
    chip = s // 2

    def ctx_peer(o):
        oc, oy, ox, oz = o % 2, (o // 2) % 4, (o // 8) % 4, o // 32
        cy, cx = (ctx // 2) % 4, (ctx // 8) % 4
        return ((((zh + oz) % 2) * 4 + (cx + ox) % 4) * 4 + (cy + oy) % 4) * 2 + (core + oc) % 2

    barrier = pltpu.get_barrier_semaphore()

    def greet(o, carry):
        pl.semaphore_signal(barrier, inc=1, device_id={"ctx": ctx_peer(o)}, device_id_type=MESH)
        return carry

    lax.fori_loop(1, 64, greet, 0)

    def greet_z(o, carry):
        pl.semaphore_signal(
            barrier,
            inc=1,
            device_id={"dp": (zl + 1 + o // 2) % 4, "ctx": (o % 2) * 32 + s},
            device_id_type=MESH,
        )
        return carry

    lax.fori_loop(0, 6, greet_z, 0)

    loads = [
        pltpu.make_async_copy(fwd_any.at[zh], fwd, tab_sem.at[0]),
        pltpu.make_async_copy(inv_any.at[zh], inv, tab_sem.at[1]),
        pltpu.make_async_copy(two_any.at[0], tab2.at[0:512, 0:512], tab_sem.at[2]),
        pltpu.make_async_copy(two_any.at[0], tab2.at[512:1024, 512:1024], tab_sem.at[3]),
        pltpu.make_async_copy(two_any.at[1], tab2.at[512:1024, 0:512], tab_sem.at[4]),
        pltpu.make_async_copy(two_any.at[2], tab2.at[0:512, 512:1024], tab_sem.at[5]),
        pltpu.make_async_copy(two_any.at[0], tab3.at[0:512, 0:512], tab_sem.at[6]),
        pltpu.make_async_copy(two_any.at[0], tab3.at[512:1024, 512:1024], tab_sem.at[7]),
        pltpu.make_async_copy(two_any.at[1], tab3.at[0:512, 512:1024], tab_sem.at[8]),
        pltpu.make_async_copy(two_any.at[2], tab3.at[512:1024, 0:512], tab_sem.at[9]),
    ]
    for load in loads:
        load.start()

    for h in range(NCH):
        for p in range(3):
            cols = w_ref[:, p * 256 + h * 128 : p * 256 + (h + 1) * 128]
            wt[h, p * 128 : (p + 1) * 128, :] = nt(perm_ref[...], cols).astype(BF)

    def project(h):
        for jj in range(2):
            mixed, smoothed = [], []
            for j in (2 * jj, 2 * jj + 1):
                xs = x_ref[j * 512 : (j + 1) * 512, :]
                rows = nt(wt[h], xs).astype(BF)
                feat[h, j] = rows
                rows = rows.astype(F32)
                mixed.append((rows[128:256] * rows[256:384]).reshape(16, 8, 512))
                gs = nt(perm_ref[...], g_ref[j * 512 : (j + 1) * 512, h * 128 : (h + 1) * 128])
                gt[h, j] = gs.astype(BF)
                smoothed.append((gs * rows[0:128]).reshape(16, 8, 512))
            for kind, pair in enumerate((mixed, smoothed)):
                even, odd = mingle(pair[0], pair[1])
                mix[kind, :, 0, jj * 8 : jj * 8 + 8, :] = even
                mix[kind, :, 1, jj * 8 : jj * 8 + 8, :] = odd
        for kind in range(2):
            block = mix[kind].reshape(32, 16, 512).astype(BF)
            send_in[h, :, kind] = block

    def offset(k):
        return (k + 31) % 63 + 1

    def in_copy(h, k):
        peer = ctx_peer(offset(k))
        return pltpu.make_async_remote_copy(
            send_in.at[h, peer // 2, peer % 2],
            recv_in.at[h, ctx],
            in_s.at[h],
            in_r.at[h],
            device_id={"ctx": peer},
            device_id_type=MESH,
        )

    def send_chunk(h):
        def step(k, carry):
            in_copy(h, k).start()
            return carry

        lax.fori_loop(0, 63, step, 0)
        recv_in[h, ctx] = send_in[h, ctx // 2, ctx % 2]

    def filter_copy(o):
        peer = zh * 32 + ctx_peer(o) % 32
        return pltpu.make_async_remote_copy(
            fsend.at[(peer // 2) % 16],
            frecv.at[s],
            fsem_s,
            fsem_r,
            device_id={"ctx": peer},
            device_id_type=MESH,
        )

    def extra_copy(o):
        peer = (1 - zh) * 32 + o
        return pltpu.make_async_remote_copy(
            fsend.at[(peer // 2) % 16],
            frecv.at[32],
            fsem_s,
            fsem_r,
            device_id={"ctx": peer},
            device_id_type=MESH,
        )

    project(0)
    pl.semaphore_wait(barrier, 69)
    send_chunk(0)

    for which, ref in enumerate((fr_in, fi_in)):
        turned = nt(eye_ref[0:16, 0:16], ref[...].astype(BF))
        for k in range(8):
            for q in range(4):
                fsc[q, pl.ds(which * 8 + k, 16, stride=16), :] = turned[
                    :, k * 512 + q * 128 : k * 512 + (q + 1) * 128
                ]
    for q in range(4):
        fsend[:, :, q * 128 : (q + 1) * 128] = fsc[q].reshape(16, 16, 128).astype(BF)

    def fstep(o, carry):
        filter_copy(o).start()
        return carry

    lax.fori_loop(1, 32, fstep, 0)
    frecv[s] = fsend[chip]

    @pl.when(s == 0)
    def _():
        def estep(o, carry):
            extra_copy(o).start()
            return carry

        lax.fori_loop(0, 32, estep, 0)

    frecv[33] = jnp.zeros((16, 512), BF)

    project(1)
    send_chunk(1)

    for j in range(4):
        xt[j] = nt(eye_ref[...], x_ref[j * 512 : (j + 1) * 512, :]).astype(BF)
    ca, sa = coarse_ref[zh, 0], coarse_ref[zh, 1]
    cb, sb = fine_ref[0][None], fine_ref[1][None]
    twc[...] = (ca * cb - sa * sb).reshape(ROWS, 512)
    tws[...] = (sa * cb + ca * sb).reshape(ROWS, 512)
    for load in loads:
        load.wait()
    pltpu.make_async_copy(frecv.at[pl.ds(0, 32)], frecv.at[pl.ds(0, 32)], fsem_r).wait()
    both = frecv[...].astype(F32)
    sign = (1 - 2 * core).astype(F32)
    fre[...] = both[:, 0:8].reshape(ROWS, 512)
    fim[...] = both[:, 8:16].reshape(ROWS, 512) * sign

    def out_copy(h, k):
        peer = ctx_peer(offset(k))
        return pltpu.make_async_remote_copy(
            send_out.at[h, peer],
            recv_out.at[h, ctx // 4, (ctx // 2) % 2, core],
            out_s.at[h],
            out_r.at[h],
            device_id={"ctx": peer},
            device_id_type=MESH,
        )

    def conv(h, carry):
        pltpu.make_async_copy(
            recv_in.at[h, pl.ds(0, 63)], recv_in.at[h, pl.ds(0, 63)], in_r.at[h]
        ).wait()
        for q in range(4):
            lanes = slice(q * 128, (q + 1) * 128)
            spec[q] = recv_in[h, :, :, lanes].astype(F32).reshape(1024, 128)
        for i in range(4):
            sig = jnp.concatenate(
                [spec[q, pl.ds(i, 256, stride=4), :] for q in range(4)], axis=1
            ).astype(BF)
            one = nn(fwd[...], sig)
            re, im = one[:ROWS], one[ROWS:]
            c, sn = twc[...], tws[...]
            prod[:, 0:512] = (re * c + im * sn).astype(BF)
            prod[:, 512:1024] = (im * c - re * sn).astype(BF)
            two = nn(prod[...], tab2[...])
            dr, di = two[:, 0:512], two[:, 512:1024]
            a, b = fre[...], fim[...]
            prod[:, 0:512] = (dr * a - di * b).astype(BF)
            prod[:, 512:1024] = (dr * b + di * a).astype(BF)
            three = nn(prod[...], tab3[...])
            er, ei = three[:, 0:512], three[:, 512:1024]
            c, sn = twc[...], tws[...]
            ret[0:ROWS, :] = (er * c - ei * sn).astype(BF)
            ret[ROWS:, :] = (ei * c + er * sn).astype(BF)
            four = nn(inv[...], ret[...])
            for q in range(4):
                spec[q, pl.ds(i, 256, stride=4), :] = four[:, q * 128 : (q + 1) * 128]
        for q in range(4):
            lanes = slice(q * 128, (q + 1) * 128)
            send_out[h, :, :, lanes] = spec[q].reshape(64, 16, 128).astype(BF)

        def step(k, inner):
            out_copy(h, k).start()
            return inner

        lax.fori_loop(0, 63, step, 0)
        recv_out[h, ctx // 4, (ctx // 2) % 2, core] = send_out[h, ctx]
        return carry

    lax.fori_loop(0, NCH, conv, 0)

    def part_copy(h, o):
        peer = zh * 32 + ctx_peer(o) % 32
        return pltpu.make_async_remote_copy(
            part.at[h, peer % 32],
            precv.at[h, s],
            p_s.at[h],
            p_r.at[h],
            device_id={"ctx": peer},
            device_id_type=MESH,
        )

    def finish(h, carry):
        pltpu.make_async_copy(
            send_out.at[h, pl.ds(0, 63)], send_out.at[h, pl.ds(0, 63)], out_r.at[h]
        ).wait()
        total = jnp.zeros((256, 384), F32)
        lanes = pl.ds(pl.multiple_of(h * 128, 128), 128)
        for jj in range(2):
            got = []
            for kind in range(2):
                even = recv_out[h, :, 0, kind].astype(F32)[:, jj * 8 : jj * 8 + 8]
                odd = recv_out[h, :, 1, kind].astype(F32)[:, jj * 8 : jj * 8 + 8]
                first, second = mingle(even, odd)
                got.append((first.reshape(128, 512), second.reshape(128, 512)))
            for q in range(2):
                j = 2 * jj + q
                smooth, mixed = got[0][q], got[1][q]
                rows = feat[h, j].astype(F32)
                gate, key, value = rows[0:128], rows[128:256], rows[256:384]
                gated = nn(permt_ref[...], (gate * smooth).astype(BF))
                out_ref[j * 512 : (j + 1) * 512, lanes] = gated.T.astype(BF)
                grads = []
                for term in (gt[h, j].astype(F32) * smooth, mixed * value, mixed * key):
                    grads.append(nn(permt_ref[...], term.astype(BF)).astype(BF))
                total = total + nt(xt[j], jnp.concatenate(grads, axis=0))
        part[h] = total.reshape(32, 8, 384)

        def step(o, inner):
            part_copy(h, o).start()
            return inner

        lax.fori_loop(1, 32, step, 0)
        precv[h, s] = part[h, s]
        return carry

    lax.fori_loop(0, NCH, finish, 0)

    for h in range(NCH):
        pltpu.make_async_copy(
            part.at[h, pl.ds(0, 31)], part.at[h, pl.ds(0, 31)], p_r.at[h]
        ).wait()
        zsend[:, h * 384 : (h + 1) * 384] = jnp.sum(precv[h], axis=0)

    owner = s // 8
    here = zh * 4 + zl

    def z_copy(half):
        return pltpu.make_async_remote_copy(
            zsend,
            zrecv.at[here],
            z_s.at[half],
            z_r,
            device_id={"dp": owner, "ctx": half * 32 + s},
            device_id_type=MESH,
        )

    for half in range(2):
        mine = (zl == owner) & (zh == half)

        @pl.when(mine)
        def _():
            zrecv[here] = zsend[...]

        @pl.when(jnp.logical_not(mine))
        def _():
            z_copy(half).start()

    def g_copy(o):
        peer = zh * 32 + ctx_peer(o) % 32
        return pltpu.make_async_remote_copy(
            fin,
            frows.at[s % 8],
            g_s,
            g_r,
            device_id={"ctx": peer},
            device_id_type=MESH,
        )

    @pl.when(zl == owner)
    def _():
        pltpu.make_async_copy(zrecv.at[pl.ds(0, 7)], zrecv.at[pl.ds(0, 7)], z_r).wait()
        fin[...] = jnp.sum(zrecv[...], axis=0) * (1.0 / math.sqrt(524288.0))

        def step(o, inner):
            g_copy(o).start()
            return inner

        lax.fori_loop(1, 32, step, 0)
        frows[s % 8] = fin[...]
        pltpu.make_async_copy(frows.at[pl.ds(0, 7)], frows.at[pl.ds(0, 7)], g_r).wait()

    @pl.when(zl != owner)
    def _():
        pltpu.make_async_copy(frows, frows, g_r).wait()

    done = frows[...].reshape(64, 768)
    for h in range(NCH):
        for p in range(3):
            grad_ref[:, p * 256 + h * 128 : p * 256 + (h + 1) * 128] = done[
                :, h * 384 + p * 128 : h * 384 + (p + 1) * 128
            ]

    for h in range(NCH):
        for buf, sem in ((recv_in, in_s), (send_out, out_s)):
            pltpu.make_async_copy(
                buf.at[h, pl.ds(0, 63)], buf.at[h, pl.ds(0, 63)], sem.at[h]
            ).wait()
        pltpu.make_async_copy(
            part.at[h, pl.ds(0, 31)], part.at[h, pl.ds(0, 31)], p_s.at[h]
        ).wait()

    pltpu.make_async_copy(frecv.at[pl.ds(0, 31)], frecv.at[pl.ds(0, 31)], fsem_s).wait()

    @pl.when(s == 0)
    def _():
        pltpu.make_async_copy(frecv.at[pl.ds(0, 32)], frecv.at[pl.ds(0, 32)], fsem_s).wait()

    for half in range(2):
        @pl.when(jnp.logical_not((zl == owner) & (zh == half)))
        def _():
            z_copy(half).wait_send()

    @pl.when(zl == owner)
    def _():
        pltpu.make_async_copy(precv.at[0, pl.ds(0, 31)], precv.at[0, pl.ds(0, 31)], g_s).wait()
        pltpu.make_async_copy(precv.at[0, pl.ds(0, 31)], precv.at[0, pl.ds(0, 31)], g_s).wait()


def per_device(inputs, grad_out, w_in, filter_real, filter_imag):
    consts = [jnp.asarray(t) for t in tables()]
    vm = pl.BlockSpec(memory_space=pltpu.VMEM)
    anyspace = pl.BlockSpec(memory_space=pl.ANY)
    v = pltpu.VMEM
    dma = pltpu.SemaphoreType.DMA
    gated, grad = pl.pallas_call(
        kernel,
        out_shape=(
            jax.ShapeDtypeStruct((2048, 256), BF),
            jax.ShapeDtypeStruct((64, 768), F32),
        ),
        in_specs=[vm] * 5 + [anyspace] * 3 + [vm] * 5,
        out_specs=(vm, vm),
        scratch_shapes=[
            v((2 * ROWS, 256), BF),
            v((256, 2 * ROWS), BF),
            v((1024, 1024), BF),
            v((1024, 1024), BF),
            v((4, 256, 512), BF),
            v((NCH, 384, 256), BF),
            v((NCH, 4, 384, 512), BF),
            v((NCH, 4, 128, 512), BF),
            v((4, 256, 128), F32),
            v((16, 16, 512), BF),
            v((34, 16, 512), BF),
            v((ROWS, 512), F32),
            v((ROWS, 512), F32),
            v((ROWS, 512), F32),
            v((ROWS, 512), F32),
            v((NCH, 32, 2, 16, 512), BF),
            v((NCH, 64, 16, 512), BF),
            v((2, 16, 2, 16, 512), F32),
            v((4, 1024, 128), F32),
            v((ROWS, 1024), BF),
            v((2 * ROWS, 512), BF),
            v((NCH, 64, 16, 512), BF),
            v((NCH, 16, 2, 2, 16, 512), BF),
            v((NCH, 32, 8, 384), F32),
            v((NCH, 32, 8, 384), F32),
            v((8, 768), F32),
            v((8, 8, 768), F32),
            v((8, 768), F32),
            v((8, 8, 768), F32),
            dma((10,)),
            dma,
            dma,
            dma((NCH,)),
            dma((NCH,)),
            dma((NCH,)),
            dma((NCH,)),
            dma((NCH,)),
            dma((NCH,)),
            dma((2,)),
            dma,
            dma,
            dma,
        ],
        name="hyena",
        compiler_params=pltpu.CompilerParams(
            collective_id=0, has_side_effects=True, vmem_limit_bytes=62 * 2**20
        ),
    )(
        inputs[0], grad_out[0], w_in,
        filter_real.reshape(4096, 16), filter_imag.reshape(4096, 16),
        *consts,
    )
    return (gated[None], grad)


def solution(mesh):
    placed = (
        P("dp", "ctx", None),
        P("dp", "ctx", None),
        P(),
        P("ctx", None, None),
        P("ctx", None, None),
    )
    return jax.shard_map(
        per_device,
        mesh=mesh,
        in_specs=placed,
        out_specs=(P("dp", "ctx", None), P("dp", None)),
        check_vma=False,
    )
```

time: 746 us -> 162 us (0.22)
  waiting for transfers between devices: 395 us -> 0 us
  starting transfers between devices: 171 us -> 0 us
  Pallas kernels: 0 us -> 152 us
  matrix products: 82.9 us -> 0 us
  local copies, waits for them, and re-layouts: 55.1 us -> 7.84 us
  other arithmetic: 21 us -> 0 us
  between operations: 14.7 us -> 0.66 us
    psum x1 -> x0, waiting for transfers between devices: 260 us -> none  [per_device(): everything = lax.psum(full_term, ('dp', 'ctx'))]
    all_to_all x8 -> x0, starting transfers between devices: 171 us -> none  [the longest x2 56 us: long_conv(): lax.all_to_all(returned, 'ctx', split_axis=1, concat_axis=0, tiled=True)]
    pallas_call x0 -> x1, Pallas kernels: none -> 152 us  [per_device(): pl.pallas_call(kernel, out_shape=(jax.ShapeDtypeStruct((2048, 256), BF),...]
    all_to_all x8 -> x0, waiting for transfers between devices: 135 us -> none  [the longest x2 47.2 us: long_conv(): lax.all_to_all(returned, 'ctx', split_axis=1, concat_axis=0, tiled=True)]
    dot_general x18 -> x0, matrix products: 82.9 us -> none  [the longest x2 15.1 us: long_conv(): jnp.einsum('fcpm,cg->fgpm', columns, cos_two, preferred_element_type=jnp....]
    another operation x10 -> x0, local copies, waits for them, and re-layouts: 27.2 us -> none  [the longest x6 18.1 us: pack_complex(): return jnp.stack([real_part, imag_part], axis=2).astype(jnp.bfloat16)]
    another operation x11 -> x0, other arithmetic: 12.4 us -> none
    reshape x4 -> x0, local copies, waits for them, and re-layouts: 10.6 us -> none  [the longest x2 6.47 us: per_device(): mixed_grid = mixed.reshape(shard_rows, N2, 2, chan_half)]
  transfers between devices with their start and end apart: 9 -> 0, of which waited for: 9 -> 0; matrix products, arithmetic and copies ran while one was open for 11% -> 0% of each run, Pallas kernels for 0% -> 0%
where the time goes in v1:
time: 162 us; the launch traced here: 161 us
  Pallas kernels  152 us (94%)
  local copies, waits for them, and re-layouts  7.84 us (5%)
    pallas_call x1, Pallas kernels, per_device(): pl.pallas_call(kernel, out_shape=(jax.ShapeDtypeStruct((2048, 256), BF),...  152 us
    unnamed x8, local copies, waits for them, and re-layouts  7.84 us

profile of v1, /device:TPU:1, one launch (start us, length us, event | category | flops | bytes accessed | tf_op | source)
XLA Modules:
  0.0 160.7 jit_solution(587458297165016641)
XLA Ops:
  0.6 0.0 copy-start
  0.6 2.9 %copy.15 = f32[8,512,16]{2,1,0:T(8,128)} copy(f32[8,512,16]{1,2,0:T(8,128)} %param.16) | data formatting | bytes 524288 | tf_op args[3]
  3.6 0.0 copy-done
  3.6 1.9 %copy.16 = f32[8,512,16]{2,1,0:T(8,128)} copy(f32[8,512,16]{1,2,0:T(8,128)S(1)} %copy-done) | data formatting | bytes 524288 | tf_op args[4]
  5.5 152.2 %hyena.1 = (bf16[2048,256]{1,0:T(8,128)(2,1)}, f32[64,768]{1,0:T(8,128)}) custom-call(bf16[2048,256]{1,0:T(8,128)(2,1)} %bitcast.7, bf16[2048,256]{1,0:T(8,128)(2,1)} %bitcast.8, bf16[256,768]{1,0:T(8,128)(2,1)} %w_ref.1, f32[4096,16]{1,0:T(8,128)} %bitcast.5, f32[4096,16]{1,0:T(8,128)} %bitcast.6, bf16[2,544,256]{2,1,0:T(8,128)(2,1)} %constant.16.clone.fwd_any, ...), custom_call_target="tpu_custom_call" | custom-call | tf_op jit(solution)/shard_map/hyena/pallas_call | solution.py:454
  157.7 0.0 copy-start.1
  157.7 2.3 %copy.19 = bf16[1,2048,256]{2,1,0:T(8,128)(2,1)} copy(bf16[1,2048,256]{2,1,0:T(8,128)(2,1)} %bitcast.9) | data formatting | bytes 2097152
  160.0 0.0 copy-done.1
  160.0 0.7 copy.20
Async XLA Ops:
  0.6 3.0 %copy-start = (f32[8,512,16]{1,2,0:T(8,128)S(1)}, f32[8,512,16]{1,2,0:T(8,128)}, u32[]{:S(2)}) copy-start(f32[8,512,16]{1,2,0:T(8,128)} %param.17) | copy-start | bytes 786436
  157.7 2.3 %copy-start.1 = (f32[64,768]{1,0:T(8,128)S(1)}, f32[64,768]{1,0:T(8,128)}, u32[]{:S(2)}) copy-start(f32[64,768]{1,0:T(8,128)} %get-tuple-element.9) | copy-start | bytes 589828

commit v2 on v1

--- a/solution.py
+++ b/solution.py
@@ -21,31 +21,33 @@
     half = N1 // 2
     period = N1 * N2
     t1 = np.arange(half)
-    fwd = np.zeros((2, 2 * ROWS, half), np.float64)
-    inv = np.zeros((2, half, 2 * ROWS), np.float64)
+    fwd = np.zeros((2 * ROWS, half), np.float64)
+    inv = np.zeros((half, 2 * ROWS), np.float64)
     base = np.zeros((2, ROWS // 8), np.int64)
     for zh in range(2):
         rows = np.concatenate(
             [zh * half + np.arange(half), (1 - zh) * half + np.arange(8), np.zeros(8, np.int64)]
         )
         base[zh] = rows[::8]
+        if zh:
+            continue
         angle = 2.0 * np.pi * ((rows[:, None] * t1[None, :]) % N1) / N1
         scale = 1.0 / math.sqrt(N1)
         cos = (np.cos(angle) * scale).astype(BF).astype(np.float64)
         sin = (np.sin(angle) * scale).astype(BF).astype(np.float64)
         cos[half + 8 :] = 0.0
         sin[half + 8 :] = 0.0
-        fwd[zh, :ROWS] = cos
-        fwd[zh, ROWS:] = -sin
+        fwd[:ROWS] = cos
+        fwd[ROWS:] = -sin
         weight = np.where((rows == 0) | (rows == half), 1.0, 2.0)
         weight[half + 1 :] = 0.0
-        inv[zh, :, :ROWS] = (weight[:, None] * cos).T
-        inv[zh, :, ROWS:] = -(weight[:, None] * sin).T
+        inv[:, :ROWS] = (weight[:, None] * cos).T
+        inv[:, ROWS:] = -(weight[:, None] * sin).T
     t2 = np.arange(N2)
     angle = 2.0 * np.pi * ((t2[:, None] * t2[None, :]) % N2) / N2
     cos2 = np.cos(angle) / math.sqrt(N2)
     sin2 = np.sin(angle) / math.sqrt(N2)
-    two = np.stack([cos2, sin2, -sin2])
+    two = np.stack([cos2, sin2])
     coarse = 2.0 * np.pi * ((base[:, :, None] * t2) % period) / period
     fine = 2.0 * np.pi * ((np.arange(8)[:, None] * t2) % period) / period
     coarse = np.stack([np.cos(coarse), np.sin(coarse)], axis=1)[:, :, :, None, :]
@@ -82,12 +84,12 @@
 
 
 def kernel(
-    x_ref, g_ref, w_ref, fr_in, fi_in, fwd_any, inv_any, two_any, coarse_ref, fine_ref,
+    x_any, g_any, w_any, fr_any, fi_any, fwd_any, inv_any, two_any, coarse_any, fine_ref,
     perm_ref, permt_ref, eye_ref,
     out_ref, grad_ref,
-    fwd, inv, tab2, tab3, xt, wt, feat, gt, fsc, fsend, frecv, fre, fim, twc, tws,
+    x_ref, g_ref, w_ref, fr_in, fi_in, coarse_ref, fwd, inv, tab2, tab3, xt, wt, feat, gt, fsc, fsend, frecv, fre, fim, twc, tws,
     send_in, recv_in, mix, spec, prod, ret, send_out, recv_out,
-    part, precv, zsend, zrecv, fin, frows,
+    part, precv, zsend, zrecv, fin, frows, smoothed,
     tab_sem, fsem_s, fsem_r, in_s, in_r, out_s, out_r, p_s, p_r, z_s, z_r, g_s, g_r,
 ):
     zl = lax.axis_index("dp")
@@ -121,21 +123,30 @@
 
     lax.fori_loop(0, 6, greet_z, 0)
 
+    inputs = [
+        pltpu.make_async_copy(w_any, w_ref, tab_sem.at[8]),
+        pltpu.make_async_copy(x_any, x_ref, tab_sem.at[9]),
+        pltpu.make_async_copy(g_any, g_ref, tab_sem.at[10]),
+        pltpu.make_async_copy(fr_any, fr_in, tab_sem.at[11]),
+        pltpu.make_async_copy(fi_any, fi_in, tab_sem.at[12]),
+        pltpu.make_async_copy(coarse_any.at[zh], coarse_ref, tab_sem.at[13]),
+    ]
+    for load in inputs:
+        load.start()
     loads = [
-        pltpu.make_async_copy(fwd_any.at[zh], fwd, tab_sem.at[0]),
-        pltpu.make_async_copy(inv_any.at[zh], inv, tab_sem.at[1]),
+        pltpu.make_async_copy(fwd_any, fwd, tab_sem.at[0]),
+        pltpu.make_async_copy(inv_any, inv, tab_sem.at[1]),
         pltpu.make_async_copy(two_any.at[0], tab2.at[0:512, 0:512], tab_sem.at[2]),
         pltpu.make_async_copy(two_any.at[0], tab2.at[512:1024, 512:1024], tab_sem.at[3]),
         pltpu.make_async_copy(two_any.at[1], tab2.at[512:1024, 0:512], tab_sem.at[4]),
-        pltpu.make_async_copy(two_any.at[2], tab2.at[0:512, 512:1024], tab_sem.at[5]),
-        pltpu.make_async_copy(two_any.at[0], tab3.at[0:512, 0:512], tab_sem.at[6]),
-        pltpu.make_async_copy(two_any.at[0], tab3.at[512:1024, 512:1024], tab_sem.at[7]),
-        pltpu.make_async_copy(two_any.at[1], tab3.at[0:512, 512:1024], tab_sem.at[8]),
-        pltpu.make_async_copy(two_any.at[2], tab3.at[512:1024, 0:512], tab_sem.at[9]),
+        pltpu.make_async_copy(two_any.at[0], tab3.at[0:512, 0:512], tab_sem.at[5]),
+        pltpu.make_async_copy(two_any.at[0], tab3.at[512:1024, 512:1024], tab_sem.at[6]),
+        pltpu.make_async_copy(two_any.at[1], tab3.at[0:512, 512:1024], tab_sem.at[7]),
     ]
     for load in loads:
         load.start()
 
+    inputs[0].wait()
     for h in range(NCH):
         for p in range(3):
             cols = w_ref[:, p * 256 + h * 128 : p * 256 + (h + 1) * 128]
@@ -143,7 +154,7 @@
 
     def project(h):
         for jj in range(2):
-            mixed, smoothed = [], []
+            mixed, turned = [], []
             for j in (2 * jj, 2 * jj + 1):
                 xs = x_ref[j * 512 : (j + 1) * 512, :]
                 rows = nt(wt[h], xs).astype(BF)
@@ -152,8 +163,8 @@
                 mixed.append((rows[128:256] * rows[256:384]).reshape(16, 8, 512))
                 gs = nt(perm_ref[...], g_ref[j * 512 : (j + 1) * 512, h * 128 : (h + 1) * 128])
                 gt[h, j] = gs.astype(BF)
-                smoothed.append((gs * rows[0:128]).reshape(16, 8, 512))
-            for kind, pair in enumerate((mixed, smoothed)):
+                turned.append((gs * rows[0:128]).reshape(16, 8, 512))
+            for kind, pair in enumerate((mixed, turned)):
                 even, odd = mingle(pair[0], pair[1])
                 mix[kind, :, 0, jj * 8 : jj * 8 + 8, :] = even
                 mix[kind, :, 1, jj * 8 : jj * 8 + 8, :] = odd
@@ -205,16 +216,20 @@
             device_id_type=MESH,
         )
 
+    inputs[1].wait()
+    inputs[2].wait()
     project(0)
     pl.semaphore_wait(barrier, 69)
     send_chunk(0)
 
+    inputs[3].wait()
+    inputs[4].wait()
     for which, ref in enumerate((fr_in, fi_in)):
-        turned = nt(eye_ref[0:16, 0:16], ref[...].astype(BF))
         for k in range(8):
+            turned = ref[k]
             for q in range(4):
                 fsc[q, pl.ds(which * 8 + k, 16, stride=16), :] = turned[
-                    :, k * 512 + q * 128 : k * 512 + (q + 1) * 128
+                    :, q * 128 : (q + 1) * 128
                 ]
     for q in range(4):
         fsend[:, :, q * 128 : (q + 1) * 128] = fsc[q].reshape(16, 16, 128).astype(BF)
@@ -241,12 +256,19 @@
 
     for j in range(4):
         xt[j] = nt(eye_ref[...], x_ref[j * 512 : (j + 1) * 512, :]).astype(BF)
-    ca, sa = coarse_ref[zh, 0], coarse_ref[zh, 1]
+    inputs[5].wait()
+    ca, sa = coarse_ref[0], coarse_ref[1]
     cb, sb = fine_ref[0][None], fine_ref[1][None]
     twc[...] = (ca * cb - sa * sb).reshape(ROWS, 512)
     tws[...] = (sa * cb + ca * sb).reshape(ROWS, 512)
     for load in loads:
         load.wait()
+    tab2[0:512, 512:1024] = -tab2[512:1024, 0:512]
+    tab3[512:1024, 0:512] = -tab3[0:512, 512:1024]
+    odd = lax.broadcasted_iota(jnp.int32, (2 * ROWS, 256), 1) % 2
+    fwd[...] = jnp.where(odd * zh == 1, -fwd[...].astype(F32), fwd[...].astype(F32)).astype(BF)
+    odd = lax.broadcasted_iota(jnp.int32, (256, 2 * ROWS), 0) % 2
+    inv[...] = jnp.where(odd * zh == 1, -inv[...].astype(F32), inv[...].astype(F32)).astype(BF)
     pltpu.make_async_copy(frecv.at[pl.ds(0, 32)], frecv.at[pl.ds(0, 32)], fsem_r).wait()
     both = frecv[...].astype(F32)
     sign = (1 - 2 * core).astype(F32)
@@ -307,23 +329,26 @@
 
     lax.fori_loop(0, NCH, conv, 0)
 
+    owner = s % 4
+    unit = s // 4
+    here = zh * 4 + zl
+
     def part_copy(h, o):
-        peer = zh * 32 + ctx_peer(o) % 32
-        return pltpu.make_async_remote_copy(
-            part.at[h, peer % 32],
+        peer = ctx_peer(o) % 32
+        return pltpu.make_async_remote_copy(
+            part.at[h, (peer % 4) * 8 + peer // 4],
             precv.at[h, s],
             p_s.at[h],
             p_r.at[h],
-            device_id={"ctx": peer},
-            device_id_type=MESH,
-        )
-
-    def finish(h, carry):
+            device_id={"ctx": zh * 32 + peer},
+            device_id_type=MESH,
+        )
+
+    def grads(h):
         pltpu.make_async_copy(
             send_out.at[h, pl.ds(0, 63)], send_out.at[h, pl.ds(0, 63)], out_r.at[h]
         ).wait()
         total = jnp.zeros((256, 384), F32)
-        lanes = pl.ds(pl.multiple_of(h * 128, 128), 128)
         for jj in range(2):
             got = []
             for kind in range(2):
@@ -334,14 +359,13 @@
             for q in range(2):
                 j = 2 * jj + q
                 smooth, mixed = got[0][q], got[1][q]
-                rows = feat[h, j].astype(F32)
-                gate, key, value = rows[0:128], rows[128:256], rows[256:384]
-                gated = nn(permt_ref[...], (gate * smooth).astype(BF))
-                out_ref[j * 512 : (j + 1) * 512, lanes] = gated.T.astype(BF)
-                grads = []
+                smoothed[j] = smooth.astype(BF)
+                rows = feat[h, j, 128:384].astype(F32)
+                key, value = rows[0:128], rows[128:256]
+                terms = []
                 for term in (gt[h, j].astype(F32) * smooth, mixed * value, mixed * key):
-                    grads.append(nn(permt_ref[...], term.astype(BF)).astype(BF))
-                total = total + nt(xt[j], jnp.concatenate(grads, axis=0))
+                    terms.append(nn(permt_ref[...], term.astype(BF)).astype(BF))
+                total = total + nt(xt[j], jnp.concatenate(terms, axis=0))
         part[h] = total.reshape(32, 8, 384)
 
         def step(o, inner):
@@ -349,74 +373,90 @@
             return inner
 
         lax.fori_loop(1, 32, step, 0)
-        precv[h, s] = part[h, s]
-        return carry
-
-    lax.fori_loop(0, NCH, finish, 0)
-
-    for h in range(NCH):
+        precv[h, s] = part[h, owner * 8 + unit]
+
+    def gates(h):
+        for j in range(4):
+            gate = feat[h, j, 0:128].astype(F32)
+            gated = (gate * smoothed[j].astype(F32)).astype(BF)
+            gated = nn(permt_ref[...], gated)
+            out_ref[j * 512 : (j + 1) * 512, h * 128 : (h + 1) * 128] = gated.T.astype(BF)
+
+    def z_copy(h, half):
+        return pltpu.make_async_remote_copy(
+            zsend.at[h],
+            zrecv.at[h, here],
+            z_s.at[h, half],
+            z_r.at[h],
+            device_id={"dp": owner, "ctx": half * 32 + s},
+            device_id_type=MESH,
+        )
+
+    def across(h):
         pltpu.make_async_copy(
             part.at[h, pl.ds(0, 31)], part.at[h, pl.ds(0, 31)], p_r.at[h]
         ).wait()
-        zsend[:, h * 384 : (h + 1) * 384] = jnp.sum(precv[h], axis=0)
-
-    owner = s // 8
-    here = zh * 4 + zl
-
-    def z_copy(half):
-        return pltpu.make_async_remote_copy(
-            zsend,
-            zrecv.at[here],
-            z_s.at[half],
-            z_r,
-            device_id={"dp": owner, "ctx": half * 32 + s},
-            device_id_type=MESH,
-        )
-
-    for half in range(2):
-        mine = (zl == owner) & (zh == half)
-
-        @pl.when(mine)
+        zsend[h] = jnp.sum(precv[h], axis=0)
+        for half in range(2):
+            mine = (zl == owner) & (zh == half)
+
+            @pl.when(mine)
+            def _():
+                zrecv[h, here] = zsend[h]
+
+            @pl.when(jnp.logical_not(mine))
+            def _():
+                z_copy(h, half).start()
+
+    def g_copy(h, o):
+        return pltpu.make_async_remote_copy(
+            fin.at[h],
+            frows.at[h, unit],
+            g_s.at[h],
+            g_r.at[h],
+            device_id={"ctx": zh * 32 + ctx_peer(o) % 32},
+            device_id_type=MESH,
+        )
+
+    def share(h):
+        @pl.when(zl == owner)
         def _():
-            zrecv[here] = zsend[...]
-
-        @pl.when(jnp.logical_not(mine))
+            pltpu.make_async_copy(
+                zrecv.at[h, pl.ds(0, 7)], zrecv.at[h, pl.ds(0, 7)], z_r.at[h]
+            ).wait()
+            fin[h] = jnp.sum(zrecv[h], axis=0) * (1.0 / math.sqrt(524288.0))
+
+            def step(o, inner):
+                g_copy(h, o).start()
+                return inner
+
+            lax.fori_loop(1, 32, step, 0)
+            frows[h, unit] = fin[h]
+
+    grads(0)
+    gates(0)
+    across(0)
+    grads(1)
+    share(0)
+    gates(1)
+    across(1)
+    share(1)
+
+    for h in range(NCH):
+        @pl.when(zl == owner)
         def _():
-            z_copy(half).start()
-
-    def g_copy(o):
-        peer = zh * 32 + ctx_peer(o) % 32
-        return pltpu.make_async_remote_copy(
-            fin,
-            frows.at[s % 8],
-            g_s,
-            g_r,
-            device_id={"ctx": peer},
-            device_id_type=MESH,
-        )
-
-    @pl.when(zl == owner)
-    def _():
-        pltpu.make_async_copy(zrecv.at[pl.ds(0, 7)], zrecv.at[pl.ds(0, 7)], z_r).wait()
-        fin[...] = jnp.sum(zrecv[...], axis=0) * (1.0 / math.sqrt(524288.0))
-
-        def step(o, inner):
-            g_copy(o).start()
-            return inner
-
-        lax.fori_loop(1, 32, step, 0)
-        frows[s % 8] = fin[...]
-        pltpu.make_async_copy(frows.at[pl.ds(0, 7)], frows.at[pl.ds(0, 7)], g_r).wait()
-
-    @pl.when(zl != owner)
-    def _():
-        pltpu.make_async_copy(frows, frows, g_r).wait()
-
-    done = frows[...].reshape(64, 768)
-    for h in range(NCH):
+            pltpu.make_async_copy(
+                frows.at[h, pl.ds(0, 7)], frows.at[h, pl.ds(0, 7)], g_r.at[h]
+            ).wait()
+
+        @pl.when(zl != owner)
+        def _():
+            pltpu.make_async_copy(frows.at[h], frows.at[h], g_r.at[h]).wait()
+
+        done = frows[h].reshape(64, 384)
         for p in range(3):
             grad_ref[:, p * 256 + h * 128 : p * 256 + (h + 1) * 128] = done[
-                :, h * 384 + p * 128 : h * 384 + (p + 1) * 128
+                :, p * 128 : (p + 1) * 128
             ]
 
     for h in range(NCH):
@@ -434,15 +474,17 @@
     def _():
         pltpu.make_async_copy(frecv.at[pl.ds(0, 32)], frecv.at[pl.ds(0, 32)], fsem_s).wait()
 
-    for half in range(2):
-        @pl.when(jnp.logical_not((zl == owner) & (zh == half)))
+    for h in range(NCH):
+        for half in range(2):
+            @pl.when(jnp.logical_not((zl == owner) & (zh == half)))
+            def _():
+                z_copy(h, half).wait_send()
+
+        @pl.when(zl == owner)
         def _():
-            z_copy(half).wait_send()
-
-    @pl.when(zl == owner)
-    def _():
-        pltpu.make_async_copy(precv.at[0, pl.ds(0, 31)], precv.at[0, pl.ds(0, 31)], g_s).wait()
-        pltpu.make_async_copy(precv.at[0, pl.ds(0, 31)], precv.at[0, pl.ds(0, 31)], g_s).wait()
+            pltpu.make_async_copy(
+                precv.at[h, pl.ds(0, 31)], precv.at[h, pl.ds(0, 31)], g_s.at[h]
+            ).wait()
 
 
 def per_device(inputs, grad_out, w_in, filter_real, filter_imag):
@@ -454,12 +496,18 @@
     gated, grad = pl.pallas_call(
         kernel,
         out_shape=(
-            jax.ShapeDtypeStruct((2048, 256), BF),
-            jax.ShapeDtypeStruct((64, 768), F32),
+            pltpu.VMEM((2048, 256), BF),
+            pltpu.VMEM((64, 768), F32),
         ),
-        in_specs=[vm] * 5 + [anyspace] * 3 + [vm] * 5,
+        in_specs=[anyspace] * 9 + [vm] * 4,
         out_specs=(vm, vm),
         scratch_shapes=[
+            v((2048, 256), BF),
+            v((2048, 256), BF),
+            v((256, 768), BF),
+            v((8, 16, 512), F32),
+            v((8, 16, 512), F32),
+            v((2, ROWS // 8, 1, 512), F32),
             v((2 * ROWS, 256), BF),
             v((256, 2 * ROWS), BF),
             v((1024, 1024), BF),
@@ -485,11 +533,12 @@
             v((NCH, 16, 2, 2, 16, 512), BF),
             v((NCH, 32, 8, 384), F32),
             v((NCH, 32, 8, 384), F32),
-            v((8, 768), F32),
-            v((8, 8, 768), F32),
-            v((8, 768), F32),
-            v((8, 8, 768), F32),
-            dma((10,)),
+            v((NCH, 8, 384), F32),
+            v((NCH, 8, 8, 384), F32),
+            v((NCH, 8, 384), F32),
+            v((NCH, 8, 8, 384), F32),
+            v((4, 128, 512), BF),
+            dma((14,)),
             dma,
             dma,
             dma((NCH,)),
@@ -498,10 +547,10 @@
             dma((NCH,)),
             dma((NCH,)),
             dma((NCH,)),
-            dma((2,)),
-            dma,
-            dma,
-            dma,
+            dma((NCH, 2)),
+            dma((NCH,)),
+            dma((NCH,)),
+            dma((NCH,)),
         ],
         name="hyena",
         compiler_params=pltpu.CompilerParams(
@@ -509,7 +558,7 @@
         ),
     )(
         inputs[0], grad_out[0], w_in,
-        filter_real.reshape(4096, 16), filter_imag.reshape(4096, 16),
+        jnp.transpose(filter_real, (0, 2, 1)), jnp.transpose(filter_imag, (0, 2, 1)),
         *consts,
     )
     return (gated[None], grad)

time: 162 us -> 151 us (0.932)
  local copies, waits for them, and re-layouts: 7.84 us -> 1.65 us
  Pallas kernels: 152 us -> 148 us
    unnamed x8 -> x2, local copies, waits for them, and re-layouts: 7.84 us -> 1.65 us
    pallas_call x1, Pallas kernels: 152 us -> 148 us  [per_device(): pl.pallas_call(kernel, out_shape=(pltpu.VMEM((2048, 256), BF), pltpu.VMEM...]
where the time goes in v2:
time: 151 us
  Pallas kernels  148 us (98%)
  local copies, waits for them, and re-layouts  1.65 us (1%)
    pallas_call x1, Pallas kernels, per_device(): pl.pallas_call(kernel, out_shape=(pltpu.VMEM((2048, 256), BF), pltpu.VMEM...  148 us

profile of v2, /device:TPU:1, one launch (start us, length us, event | category | flops | bytes accessed | tf_op | source)
XLA Modules:
  0.0 150.8 jit_solution(2813341663786386923)
XLA Ops:
  0.6 148.5 %hyena.1 = (bf16[2048,256]{1,0:T(8,128)(2,1)S(1)}, f32[64,768]{1,0:T(8,128)S(1)}) custom-call(bf16[2048,256]{1,0:T(8,128)(2,1)} %bitcast.6, bf16[2048,256]{1,0:T(8,128)(2,1)} %bitcast.7, bf16[256,768]{1,0:T(8,128)(2,1)} %w_any.1, f32[8,16,512]{2,1,0:T(8,128)} %bitcast.8, f32[8,16,512]{2,1,0:T(8,128)} %bitcast.9, bf16[544,256]{1,0:T(8,128)(2,1)} %constant.16.clone.fwd_any, ...), custom_call_target="tpu_custom_call" | custom-call | tf_op jit(solution)/shard_map/hyena/pallas_call | solution.py:496
  149.1 1.0 copy.17
  150.1 0.7 copy.18

commit v3 on v2

--- a/solution.py
+++ b/solution.py
@@ -281,7 +281,7 @@
             send_out.at[h, peer],
             recv_out.at[h, ctx // 4, (ctx // 2) % 2, core],
             out_s.at[h],
-            out_r.at[h],
+            out_r.at[h, offset(k) // 32],
             device_id={"ctx": peer},
             device_id_type=MESH,
         )
@@ -333,47 +333,54 @@
     unit = s // 4
     here = zh * 4 + zl
 
-    def part_copy(h, o):
+    def part_copy(h, half, o):
         peer = ctx_peer(o) % 32
         return pltpu.make_async_remote_copy(
-            part.at[h, (peer % 4) * 8 + peer // 4],
-            precv.at[h, s],
-            p_s.at[h],
-            p_r.at[h],
+            part.at[h, half, (peer % 4) * 8 + peer // 4],
+            precv.at[h, half, s],
+            p_s.at[h, half],
+            p_r.at[h, half],
             device_id={"ctx": zh * 32 + peer},
             device_id_type=MESH,
         )
 
-    def grads(h):
+    def grads(h, cross):
+        count = 31 + cross
         pltpu.make_async_copy(
-            send_out.at[h, pl.ds(0, 63)], send_out.at[h, pl.ds(0, 63)], out_r.at[h]
+            send_out.at[h, pl.ds(0, count)], send_out.at[h, pl.ds(0, count)], out_r.at[h, cross]
         ).wait()
-        total = jnp.zeros((256, 384), F32)
+        half = (zh + cross) % 2
+        eight = pl.ds(pl.multiple_of(half * 8, 8), 8)
+        here64 = pl.ds(pl.multiple_of(half * 64, 64), 64)
+        keys = pl.ds(pl.multiple_of(128 + half * 64, 64), 64)
+        values = pl.ds(pl.multiple_of(256 + half * 64, 64), 64)
+        back = permt_ref[0:64, 0:64]
+        total = jnp.zeros((256, 192), F32)
         for jj in range(2):
             got = []
             for kind in range(2):
-                even = recv_out[h, :, 0, kind].astype(F32)[:, jj * 8 : jj * 8 + 8]
-                odd = recv_out[h, :, 1, kind].astype(F32)[:, jj * 8 : jj * 8 + 8]
+                even = recv_out[h, eight, 0, kind].astype(F32)[:, jj * 8 : jj * 8 + 8]
+                odd = recv_out[h, eight, 1, kind].astype(F32)[:, jj * 8 : jj * 8 + 8]
                 first, second = mingle(even, odd)
-                got.append((first.reshape(128, 512), second.reshape(128, 512)))
+                got.append((first.reshape(64, 512), second.reshape(64, 512)))
             for q in range(2):
                 j = 2 * jj + q
                 smooth, mixed = got[0][q], got[1][q]
-                smoothed[j] = smooth.astype(BF)
-                rows = feat[h, j, 128:384].astype(F32)
-                key, value = rows[0:128], rows[128:256]
+                smoothed[j, here64] = smooth.astype(BF)
+                key = feat[h, j, keys].astype(F32)
+                value = feat[h, j, values].astype(F32)
                 terms = []
-                for term in (gt[h, j].astype(F32) * smooth, mixed * value, mixed * key):
-                    terms.append(nn(permt_ref[...], term.astype(BF)).astype(BF))
+                for term in (gt[h, j, here64].astype(F32) * smooth, mixed * value, mixed * key):
+                    terms.append(nn(back, term.astype(BF)).astype(BF))
                 total = total + nt(xt[j], jnp.concatenate(terms, axis=0))
-        part[h] = total.reshape(32, 8, 384)
+        part[h, half] = total.reshape(32, 8, 192).astype(BF)
 
         def step(o, inner):
-            part_copy(h, o).start()
+            part_copy(h, half, o).start()
             return inner
 
         lax.fori_loop(1, 32, step, 0)
-        precv[h, s] = part[h, owner * 8 + unit]
+        precv[h, half, s] = part[h, half, owner * 8 + unit]
 
     def gates(h):
         for j in range(4):
@@ -393,10 +400,10 @@
         )
 
     def across(h):
-        pltpu.make_async_copy(
-            part.at[h, pl.ds(0, 31)], part.at[h, pl.ds(0, 31)], p_r.at[h]
-        ).wait()
-        zsend[h] = jnp.sum(precv[h], axis=0)
+        for half in range(2):
+            block = part.at[h, half, pl.ds(0, 31)]
+            pltpu.make_async_copy(block, block, p_r.at[h, half]).wait()
+            zsend[h, half] = jnp.sum(precv[h, half].astype(F32), axis=0)
         for half in range(2):
             mine = (zl == owner) & (zh == half)
 
@@ -433,10 +440,12 @@
             lax.fori_loop(1, 32, step, 0)
             frows[h, unit] = fin[h]
 
-    grads(0)
+    grads(0, 0)
+    grads(0, 1)
     gates(0)
     across(0)
-    grads(1)
+    grads(1, 0)
+    grads(1, 1)
     share(0)
     gates(1)
     across(1)
@@ -453,20 +462,23 @@
         def _():
             pltpu.make_async_copy(frows.at[h], frows.at[h], g_r.at[h]).wait()
 
-        done = frows[h].reshape(64, 384)
         for p in range(3):
-            grad_ref[:, p * 256 + h * 128 : p * 256 + (h + 1) * 128] = done[
-                :, p * 128 : (p + 1) * 128
-            ]
+            grad_ref[:, p * 256 + h * 128 : p * 256 + (h + 1) * 128] = jnp.concatenate(
+                [
+                    frows[h, :, half].reshape(64, 192)[:, p * 64 : (p + 1) * 64]
+                    for half in range(2)
+                ],
+                axis=1,
+            )
 
     for h in range(NCH):
         for buf, sem in ((recv_in, in_s), (send_out, out_s)):
             pltpu.make_async_copy(
                 buf.at[h, pl.ds(0, 63)], buf.at[h, pl.ds(0, 63)], sem.at[h]
             ).wait()
-        pltpu.make_async_copy(
-            part.at[h, pl.ds(0, 31)], part.at[h, pl.ds(0, 31)], p_s.at[h]
-        ).wait()
+        for half in range(2):
+            block = part.at[h, half, pl.ds(0, 31)]
+            pltpu.make_async_copy(block, block, p_s.at[h, half]).wait()
 
     pltpu.make_async_copy(frecv.at[pl.ds(0, 31)], frecv.at[pl.ds(0, 31)], fsem_s).wait()
 
@@ -482,9 +494,8 @@
 
         @pl.when(zl == owner)
         def _():
-            pltpu.make_async_copy(
-                precv.at[h, pl.ds(0, 31)], precv.at[h, pl.ds(0, 31)], g_s.at[h]
-            ).wait()
+            for _ in range(31):
+                pltpu.make_async_copy(fin.at[h], fin.at[h], g_s.at[h]).wait()
 
 
 def per_device(inputs, grad_out, w_in, filter_real, filter_imag):
@@ -531,12 +542,12 @@
             v((2 * ROWS, 512), BF),
             v((NCH, 64, 16, 512), BF),
             v((NCH, 16, 2, 2, 16, 512), BF),
-            v((NCH, 32, 8, 384), F32),
-            v((NCH, 32, 8, 384), F32),
-            v((NCH, 8, 384), F32),
-            v((NCH, 8, 8, 384), F32),
-            v((NCH, 8, 384), F32),
-            v((NCH, 8, 8, 384), F32),
+            v((NCH, 2, 32, 8, 192), BF),
+            v((NCH, 2, 32, 8, 192), BF),
+            v((NCH, 2, 8, 192), F32),
+            v((NCH, 8, 2, 8, 192), F32),
+            v((NCH, 2, 8, 192), F32),
+            v((NCH, 8, 2, 8, 192), F32),
             v((4, 128, 512), BF),
             dma((14,)),
             dma,
@@ -544,9 +555,9 @@
             dma((NCH,)),
             dma((NCH,)),
             dma((NCH,)),
-            dma((NCH,)),
-            dma((NCH,)),
-            dma((NCH,)),
+            dma((NCH, 2)),
+            dma((NCH, 2)),
+            dma((NCH, 2)),
             dma((NCH, 2)),
             dma((NCH,)),
             dma((NCH,)),

time: 151 us -> 147 us (0.974)
  Pallas kernels: 148 us -> 145 us
    pallas_call x1, Pallas kernels: 148 us -> 145 us  [per_device(): pl.pallas_call(kernel, out_shape=(pltpu.VMEM((2048, 256), BF), pltpu.VMEM...]
where the time goes in v3:
time: 147 us
  Pallas kernels  145 us (99%)
  local copies, waits for them, and re-layouts  1.65 us (1%)
    pallas_call x1, Pallas kernels, per_device(): pl.pallas_call(kernel, out_shape=(pltpu.VMEM((2048, 256), BF), pltpu.VMEM...  145 us

profile of v3, /device:TPU:1, one launch (start us, length us, event | category | flops | bytes accessed | tf_op | source)
XLA Modules:
  0.0 147.4 jit_solution(6367626129892855767)
XLA Ops:
  0.6 145.1 %hyena.1 = (bf16[2048,256]{1,0:T(8,128)(2,1)S(1)}, f32[64,768]{1,0:T(8,128)S(1)}) custom-call(bf16[2048,256]{1,0:T(8,128)(2,1)} %bitcast.6, bf16[2048,256]{1,0:T(8,128)(2,1)} %bitcast.7, bf16[256,768]{1,0:T(8,128)(2,1)} %w_any.1, f32[8,16,512]{2,1,0:T(8,128)} %bitcast.8, f32[8,16,512]{2,1,0:T(8,128)} %bitcast.9, bf16[544,256]{1,0:T(8,128)(2,1)} %constant.16.clone.fwd_any, ...), custom_call_target="tpu_custom_call" | custom-call | tf_op jit(solution)/shard_map/hyena/pallas_call | solution.py:507
  145.7 1.0 copy.17
  146.7 0.7 copy.18

commit v4 on v3

--- a/solution.py
+++ b/solution.py
@@ -87,10 +87,10 @@
     x_any, g_any, w_any, fr_any, fi_any, fwd_any, inv_any, two_any, coarse_any, fine_ref,
     perm_ref, permt_ref, eye_ref,
     out_ref, grad_ref,
-    x_ref, g_ref, w_ref, fr_in, fi_in, coarse_ref, fwd, inv, tab2, tab3, xt, wt, feat, gt, fsc, fsend, frecv, fre, fim, twc, tws,
+    x_ref, g_ref, w_ref, fr_in, fi_in, coarse_ref, fwd, inv, tab2, tab3, xt, wt, feat, gt, fsc, fsend, frecv, esc, esend, erecv, fre, fim, twc, tws,
     send_in, recv_in, mix, spec, prod, ret, send_out, recv_out,
     part, precv, zsend, zrecv, fin, frows, smoothed,
-    tab_sem, fsem_s, fsem_r, in_s, in_r, out_s, out_r, p_s, p_r, z_s, z_r, g_s, g_r,
+    tab_sem, e_s, e_r, fsem_s, fsem_r, in_s, in_r, out_s, out_r, p_s, p_r, z_s, z_r, g_s, g_r,
 ):
     zl = lax.axis_index("dp")
     ctx = lax.axis_index("ctx")
@@ -208,10 +208,10 @@
     def extra_copy(o):
         peer = (1 - zh) * 32 + o
         return pltpu.make_async_remote_copy(
-            fsend.at[(peer // 2) % 16],
-            frecv.at[32],
-            fsem_s,
-            fsem_r,
+            esend.at[(peer // 2) % 16],
+            erecv,
+            e_s,
+            e_r,
             device_id={"ctx": peer},
             device_id_type=MESH,
         )
@@ -234,6 +234,11 @@
     for q in range(4):
         fsend[:, :, q * 128 : (q + 1) * 128] = fsc[q].reshape(16, 16, 128).astype(BF)
 
+    for which, ref in enumerate((fr_in, fi_in)):
+        for q in range(4):
+            esc[pl.ds(which * 4 + q, 16, stride=8), :] = ref[0][:, q * 128 : (q + 1) * 128]
+    esend[...] = esc[...].reshape(16, 8, 128).astype(BF)
+
     def fstep(o, carry):
         filter_copy(o).start()
         return carry
@@ -249,7 +254,6 @@
 
         lax.fori_loop(0, 32, estep, 0)
 
-    frecv[33] = jnp.zeros((16, 512), BF)
 
     project(1)
     send_chunk(1)
@@ -269,11 +273,19 @@
     fwd[...] = jnp.where(odd * zh == 1, -fwd[...].astype(F32), fwd[...].astype(F32)).astype(BF)
     odd = lax.broadcasted_iota(jnp.int32, (256, 2 * ROWS), 0) % 2
     inv[...] = jnp.where(odd * zh == 1, -inv[...].astype(F32), inv[...].astype(F32)).astype(BF)
-    pltpu.make_async_copy(frecv.at[pl.ds(0, 32)], frecv.at[pl.ds(0, 32)], fsem_r).wait()
+    pltpu.make_async_copy(frecv.at[pl.ds(0, 31)], frecv.at[pl.ds(0, 31)], fsem_r).wait()
+    pltpu.make_async_copy(erecv, erecv, e_r).wait()
     both = frecv[...].astype(F32)
     sign = (1 - 2 * core).astype(F32)
-    fre[...] = both[:, 0:8].reshape(ROWS, 512)
-    fim[...] = both[:, 8:16].reshape(ROWS, 512) * sign
+    fre[0:256] = both[:, 0:8].reshape(256, 512)
+    fim[0:256] = both[:, 8:16].reshape(256, 512) * sign
+    more = erecv[...].astype(F32)
+    for q in range(4):
+        lanes = slice(q * 128, (q + 1) * 128)
+        fre[256:264, lanes] = jnp.broadcast_to(more[q : q + 1], (8, 128))
+        fim[256:264, lanes] = jnp.broadcast_to(more[q + 4 : q + 5], (8, 128)) * sign
+    fre[264:ROWS] = jnp.zeros((8, 512), F32)
+    fim[264:ROWS] = jnp.zeros((8, 512), F32)
 
     def out_copy(h, k):
         peer = ctx_peer(offset(k))
@@ -484,7 +496,8 @@
 
     @pl.when(s == 0)
     def _():
-        pltpu.make_async_copy(frecv.at[pl.ds(0, 32)], frecv.at[pl.ds(0, 32)], fsem_s).wait()
+        pltpu.make_async_copy(esend, esend, e_s).wait()
+        pltpu.make_async_copy(esend, esend, e_s).wait()
 
     for h in range(NCH):
         for half in range(2):
@@ -529,7 +542,10 @@
             v((NCH, 4, 128, 512), BF),
             v((4, 256, 128), F32),
             v((16, 16, 512), BF),
-            v((34, 16, 512), BF),
+            v((32, 16, 512), BF),
+            v((128, 128), F32),
+            v((16, 8, 128), BF),
+            v((8, 128), BF),
             v((ROWS, 512), F32),
             v((ROWS, 512), F32),
             v((ROWS, 512), F32),
@@ -550,6 +566,8 @@
             v((NCH, 8, 2, 8, 192), F32),
             v((4, 128, 512), BF),
             dma((14,)),
+            dma,
+            dma,
             dma,
             dma,
             dma((NCH,)),

time: 147 us -> 140 us (0.952)
  Pallas kernels: 145 us -> 137 us
    pallas_call x1, Pallas kernels: 145 us -> 137 us  [per_device(): pl.pallas_call(kernel, out_shape=(pltpu.VMEM((2048, 256), BF), pltpu.VMEM...]
where the time goes in v4:
time: 140 us
  Pallas kernels  137 us (98%)
  local copies, waits for them, and re-layouts  1.65 us (1%)
    pallas_call x1, Pallas kernels, per_device(): pl.pallas_call(kernel, out_shape=(pltpu.VMEM((2048, 256), BF), pltpu.VMEM...  137 us

profile of v4, /device:TPU:1, one launch (start us, length us, event | category | flops | bytes accessed | tf_op | source)
XLA Modules:
  0.0 139.7 jit_solution(12330848326836106153)
XLA Ops:
  0.6 137.4 %hyena.1 = (bf16[2048,256]{1,0:T(8,128)(2,1)S(1)}, f32[64,768]{1,0:T(8,128)S(1)}) custom-call(bf16[2048,256]{1,0:T(8,128)(2,1)} %bitcast.6, bf16[2048,256]{1,0:T(8,128)(2,1)} %bitcast.7, bf16[256,768]{1,0:T(8,128)(2,1)} %w_any.1, f32[8,16,512]{2,1,0:T(8,128)} %bitcast.8, f32[8,16,512]{2,1,0:T(8,128)} %bitcast.9, bf16[544,256]{1,0:T(8,128)(2,1)} %constant.16.clone.fwd_any, ...), custom_call_target="tpu_custom_call" | custom-call | tf_op jit(solution)/shard_map/hyena/pallas_call | solution.py:520
  138.0 1.0 copy.17
  139.0 0.7 copy.18
